TPU v7x, 256 devices: a whole 4x4x8 slice. The times are simulated.
256 devices in a mesh: seq: 64 (over x, z, core), head: 4 (over y).
Axes of the slice: x: 4, y: 4, z: 8, core: 2. Of those that a mesh axis runs over, the one named last changes fastest.
Arguments:
- latent: bfloat16 [64, 16, 1024], P('seq'), may hold values from -6 to 6
- stem_weight: bfloat16 [192, 3072], replicated, may hold values from -0.4375 to 0.4375
- stem_bias: float32 [3072], replicated, may hold values from -6 to 6
- mod_shift: float32 [3072], replicated, may hold values from -3 to 3
- mod_scale: float32 [3072], replicated, may hold values from -3 to 3
- qkv_weight: bfloat16 [3072, 3, 12, 128], P(None, None, 'head'), may hold values from -0.109375 to 0.109375
- q_gain: float32 [128], replicated, may hold values from 0.1 to 1.9
- k_gain: float32 [128], replicated, may hold values from 0.1 to 1.9
- tile_lists: int32 [128, 4], replicated, may hold values from 0 to 127, as said below
- out_grad: bfloat16 [16384, 12, 128], P('seq', 'head'), may hold values from -0.125 to 0.125
Outputs:
- qkv_weight_grad: float32 [3072, 3, 12, 128], P('seq', None, 'head')
- stem_weight_grad: float32 [192, 3072], P(None, 'head')
- vector_grad: float32 [3, 3072], P(None, 'head')
Inputs may be any that keep to these rules, and one draw needn't show every extreme that they name: `tile_lists`: row b holds 4 different tiles of tile b's own group of 8 tiles (b - b % 8 to b - b % 8 + 7), the first being b itself.
All inputs are finite; a program needn't handle non-finite values.
Results may differ from a plain program's by a relative error of at most 0.0078.
Values may be sent and summed in bfloat16 or wider, within the bound.
No kernel may reach another device: no remote copies, remote signals or barrier semaphores. Data moves between devices by JAX's collectives and lax.ppermute only.
A program may use at most 128 MiB of HBM per device.

v0:
```python
import jax
import jax.numpy as jnp
from jax import lax
from jax.sharding import PartitionSpec as P

TT = 2
TS = 8
KNB = 4
HG = 32
WG = 16
ln_eps = 1e-06


def swapped(value, axis, distance):
    mask = 2**distance
    pairs = [(source, source ^ mask) for source in range(lax.axis_size(axis))]
    return lax.ppermute(value, axis, pairs)


def from_behind(value, axis, steps):
    count = lax.axis_size(axis)
    first, last = (max(0, -steps), min(count, count - steps))
    return lax.ppermute(value, axis, [(source, source + steps) for source in range(first, last)])


def frames_to_tiles(blocks, row_total, col_total, tile_side):
    frames = blocks.shape[0]
    remain = blocks.shape[2:]
    shaped = blocks.reshape(
        (frames, row_total // tile_side, tile_side, col_total // tile_side, tile_side) + remain
    )
    shaped = jnp.transpose(shaped, (1, 3, 0, 2, 4) + tuple(range(5, 5 + len(remain))))
    return shaped.reshape(
        (row_total // tile_side * (col_total // tile_side), frames * tile_side * tile_side) + remain
    )


def tiles_to_frames(blocks, frames, row_total, col_total, tile_side):
    remain = blocks.shape[2:]
    shaped = blocks.reshape(
        (row_total // tile_side, col_total // tile_side, frames, tile_side, tile_side) + remain
    )
    shaped = jnp.transpose(shaped, (2, 0, 3, 1, 4) + tuple(range(5, 5 + len(remain))))
    return shaped.reshape((frames, row_total * col_total) + remain)


def qk_norm(raw_values, gain_vector):
    return (
        raw_values
        * lax.rsqrt(jnp.mean(raw_values * raw_values, -1, keepdims=True) + ln_eps)
        * gain_vector
    )


def norm_back(feature_grad, normed, inv_std, mod_scale):
    scaled = feature_grad * (1.0 + mod_scale)
    return (
        scaled
        - jnp.mean(scaled, -1, keepdims=True)
        - normed * jnp.mean(scaled * normed, -1, keepdims=True)
    ) * inv_std


def attend(queries, out_grads, key_vals, values, score_scale):
    scores = (
        jnp.einsum("brhe,bmhe->bhrm", queries, key_vals, preferred_element_type=jnp.float32)
        * score_scale
    )
    weights = jnp.exp(scores)
    probability = weights / jnp.sum(weights, axis=-1, keepdims=True)
    rounded = probability.astype(jnp.bfloat16)
    slopes = jnp.einsum("brhe,bmhe->bhrm", out_grads, values, preferred_element_type=jnp.float32)
    centre = jnp.sum(probability * slopes, axis=-1, keepdims=True)
    shaped = (probability * (slopes - centre)).astype(jnp.bfloat16)
    query_grad = (
        jnp.einsum("bhrm,bmhe->brhe", shaped, key_vals, preferred_element_type=jnp.float32)
        * score_scale
    )
    key_grad = (
        jnp.einsum("bhrm,brhe->bmhe", shaped, queries, preferred_element_type=jnp.float32)
        * score_scale
    )
    value_grad = jnp.einsum(
        "bhrm,brhe->bmhe", rounded, out_grads, preferred_element_type=jnp.float32
    )
    return (query_grad, key_grad, value_grad)


def group_share(blocks):
    seq_place = lax.axis_index("seq")
    for bit_index in range((2 * TT).bit_length() - 1):
        partner = swapped(blocks, "seq", bit_index)
        is_lower = seq_place // (1 << bit_index) % 2 == 0
        first_half = jnp.where(is_lower, blocks, partner)
        second_half = jnp.where(is_lower, partner, blocks)
        blocks = jnp.concatenate([first_half, second_half], 0)
    return blocks


def group_return(blocks):
    seq_place = lax.axis_index("seq")
    for bit_index in reversed(range((2 * TT).bit_length() - 1)):
        half_size = blocks.shape[0] // 2
        is_lower = seq_place // (1 << bit_index) % 2 == 0
        kept_part = jnp.where(is_lower, blocks[:half_size], blocks[half_size:])
        sent_part = jnp.where(is_lower, blocks[half_size:], blocks[:half_size])
        blocks = kept_part + swapped(sent_part, "seq", bit_index)
    return blocks[0]


def seq_total(stem_part, vector_part):
    return lax.psum((stem_part, vector_part), "seq")


def per_device(
    latent,
    stem_weight,
    stem_bias,
    mod_shift,
    mod_scale,
    qkv_weight,
    q_gain,
    k_gain,
    tile_lists,
    out_grad,
):
    half_rows = HG // 2
    tok_count = half_rows * WG
    frame_tokens = HG * WG
    model_width = qkv_weight.shape[0]
    heads_here = qkv_weight.shape[2]
    head_dim = qkv_weight.shape[3]
    score_scale = head_dim ** (-0.5)
    before = from_behind(latent, "seq", 2)
    after = from_behind(latent, "seq", -2)
    padded = jnp.concatenate([before, latent, after], 0)
    channels = latent.shape[1]
    patches = padded.reshape(3, channels, half_rows, 2, WG, 2)
    patches = jnp.transpose(patches, (2, 4, 0, 1, 3, 5)).reshape(tok_count, 12 * channels)
    embedded = jnp.dot(patches, stem_weight, preferred_element_type=jnp.float32) + stem_bias
    centred = embedded - jnp.mean(embedded, -1, keepdims=True)
    inv_std = lax.rsqrt(jnp.mean(centred * centred, -1, keepdims=True) + ln_eps)
    normed = centred * inv_std
    hidden = (normed * (1.0 + mod_scale) + mod_shift).astype(jnp.bfloat16)
    columns = 3 * heads_here * head_dim
    flat_weight = qkv_weight.reshape(model_width, columns)
    projected = jnp.dot(hidden, flat_weight, preferred_element_type=jnp.float32).reshape(
        tok_count, 3, heads_here, head_dim
    )
    q_normed, q_back = jax.vjp(lambda raw_values: qk_norm(raw_values, q_gain), projected[:, 0])
    k_normed, k_back = jax.vjp(lambda raw_values: qk_norm(raw_values, k_gain), projected[:, 1])
    queries = q_normed.astype(jnp.bfloat16)
    key_vals = k_normed.astype(jnp.bfloat16)
    values = projected[:, 2].astype(jnp.bfloat16)
    seq_place = lax.axis_index("seq")
    group_devs = 2 * TT
    my_group = seq_place // group_devs
    my_half = seq_place % 2
    tiles_group = HG // TS * (WG // TS)
    half_tiles = tiles_group // 2
    local_lists = (
        lax.dynamic_slice_in_dim(tile_lists, my_group * tiles_group, tiles_group, 0)
        - my_group * tiles_group
    )
    shared = group_share(jnp.stack([key_vals, values], 1)[None])
    shared = shared.reshape((TT, frame_tokens) + shared.shape[2:])
    tiles = frames_to_tiles(shared, HG, WG, TS)
    tile_len = tiles.shape[1]
    my_lists = lax.dynamic_slice_in_dim(local_lists, my_half * half_tiles, half_tiles, 0)
    near_tiles = jnp.take(tiles, my_lists.reshape(-1), axis=0)
    near_tiles = near_tiles.reshape(half_tiles, KNB * tile_len, 2, heads_here, head_dim)
    own_queries = frames_to_tiles(queries[None], half_rows, WG, TS)
    own_grads = frames_to_tiles(out_grad[None], half_rows, WG, TS)
    query_part, key_part, value_part = attend(
        own_queries, own_grads, near_tiles[:, :, 0], near_tiles[:, :, 1], score_scale
    )
    query_grad = tiles_to_frames(query_part, 1, half_rows, WG, TS)[0]
    pair_part = jnp.stack([key_part, value_part], 2).reshape(
        half_tiles * KNB, tile_len, 2, heads_here, head_dim
    )
    pair_tiles = (
        jnp.zeros((tiles_group, tile_len, 2, heads_here, head_dim), jnp.float32)
        .at[my_lists.reshape(-1)]
        .add(pair_part)
    )
    framed = tiles_to_frames(pair_tiles, TT, HG, WG, TS)
    returned = group_return(framed.reshape((group_devs, tok_count) + framed.shape[2:]))
    key_grad = returned[:, 0]
    value_grad = returned[:, 1]
    raw_q = q_back(query_grad)[0]
    raw_k = k_back(key_grad)[0]
    mixed_grad = (
        jnp.stack([raw_q, raw_k, value_grad], 1).astype(jnp.bfloat16).reshape(tok_count, columns)
    )
    weight_grad = lax.psum_scatter(
        lax.dot_general(
            hidden, mixed_grad, (((0,), (0,)), ((), ())), preferred_element_type=jnp.float32
        ),
        "seq",
        scatter_dimension=0,
        tiled=True,
    )
    weight_grad = weight_grad.reshape(-1, 3, heads_here, head_dim)
    feature_grad = lax.dot_general(
        mixed_grad, flat_weight, (((1,), (1,)), ((), ())), preferred_element_type=jnp.float32
    )
    patch_rows = patches.astype(jnp.float32)
    feature_grad = lax.psum(feature_grad, "head")
    embed_grad = norm_back(feature_grad, normed, inv_std, mod_scale)
    share_cols = model_width // lax.axis_size("head")
    offset = lax.axis_index("head") * share_cols
    grad_slice = lax.dynamic_slice_in_dim(feature_grad, offset, share_cols, 1)
    normed_slice = lax.dynamic_slice_in_dim(normed, offset, share_cols, 1)
    embed_slice = lax.dynamic_slice_in_dim(embed_grad, offset, share_cols, 1)
    stem_part = lax.dot_general(
        patch_rows, embed_slice, (((0,), (0,)), ((), ())), precision=lax.Precision.HIGHEST
    )
    vector_part = jnp.stack(
        [jnp.sum(grad_slice, 0), jnp.sum(grad_slice * normed_slice, 0), jnp.sum(embed_slice, 0)]
    )
    stem_grad, vector_grad = seq_total(stem_part, vector_part)
    return (weight_grad, stem_grad, vector_grad)


def solution(mesh):
    return jax.shard_map(
        per_device,
        mesh=mesh,
        in_specs=(
            P("seq", None, None),
            P(),
            P(),
            P(),
            P(),
            P(None, None, "head", None),
            P(),
            P(),
            P(),
            P("seq", "head", None),
        ),
        out_specs=(P("seq", None, "head", None), P(None, "head"), P(None, "head")),
        check_vma=False,
    )
```

profile of v0, /device:TPU:8, one launch (start us, length us, event | category | flops | bytes accessed | tf_op | source)
XLA Modules:
  0.0 514.7 jit_solution(13901229938263370222)
XLA Ops:
  8.1 4.0 collective-permute-start
  12.0 1.3 collective-permute-start.1
  13.3 0.7 broadcast_add_fusion
  14.0 10.3 %copy.44 = bf16[3072,3,3,128]{0,3,2,1:T(8,128)(2,1)} copy(bf16[3072,3,3,128]{3,0,2,1:T(8,128)(2,1)} %param.15) | data formatting | bytes 14155776 | tf_op args[5]
  24.7 1.7 copy.42
  26.4 0.7 reshape.189
  27.1 0.7 fusion.29
  28.3 1.1 copy-done.2
  29.4 0.5 subtract_multiply_fusion
  30.4 0.9 slice-done.3
  31.3 2.3 fusion
  34.0 0.7 copy-done.8
  35.6 1.1 collective-permute-done.2
  36.9 2.9 collective-permute-start.3
  40.2 17.6 %collective-permute-done.3 = bf16[2,256,2,3,128]{4,1,3,2,0:T(8,128)(2,1)} collective-permute-done((bf16[2,256,2,3,128]{4,1,3,2,0:T(8,128)(2,1)S(1)}, bf16[2,256,2,3,128]{4,1,3,2,0:T(8,128)(2,1)}, u32[]{:S(2)}, u32[]{:S(2)}) %collective-permute-start.3) | collective-permute-done | bytes 786464 | tf_op jit(solution)/shard_map/ppermute | solution.py:17
  57.7 1.2 broadcast_select_fusion.1
  59.7 2.6 gather_fusion
  62.3 2.3 copy.48
  64.6 0.5 copy_select_fusion
  65.1 0.7 fusion.2
  65.8 1.0 copy-done.6
  66.8 0.7 multiply_exponential_fusion
  67.5 3.3 convolution_bitcast_fusion.1
  70.8 2.1 fusion.4
  73.0 1.9 copy.54
  75.2 0.9 copy-done.11
  76.0 0.6 multiply_bitcast_fusion
  76.7 2.3 copy.53
  79.0 3.3 pad_maximum_fusion
  82.3 3.1 copy.55
  85.7 9.3 %scatter_fusion = f32[8,128,2,3,128]{4,1,3,2,0:T(8,128)S(1)} fusion(f32[8,128,2,3,128]{4,1,3,2,0:T(8,128)S(1)} %broadcast_in_dim.47, s32[16]{0:T(128)S(1)} %fusion.24, f32[16,128,2,3,128]{4,1,3,2,0:T(8,128)} %copy.55), kind=kCustom, calls=%fused_computation.1 | custom fusion | flops 1572864 | bytes 18874432 | tf_op jit(solution)/shard_map/scatter-add | solution.py:184
  95.9 1.8 collective-permute-start.4
  97.7 34.2 %collective-permute-done.4 = f32[2,256,2,3,128]{4,1,3,2,0:T(8,128)S(1)} collective-permute-done((f32[2,256,2,3,128]{4,1,3,2,0:T(8,128)S(1)}, f32[2,256,2,3,128]{4,1,3,2,0:T(8,128)S(1)}, u32[]{:S(2)}, u32[]{:S(2)}) %collective-permute-start.4) | collective-permute-done | bytes 1572896 | tf_op jit(solution)/shard_map/ppermute | solution.py:17
  132.3 1.8 copy-done.7
  135.6 0.6 copy-done.13
  136.3 4.0 convolution_bitcast_fusion
  140.6 2.1 maximum_convert_fusion
  142.7 2.1 copy.59
  144.8 8.4 %fusion.14 = f32[3072,1152]{1,0:T(8,128)} fusion(bf16[256,1152]{0,1:T(8,128)(2,1)} %bitcast.148, f32[256,3072]{1,0:T(8,128)S(1)} %copy-done.5, f32[3072]{0:T(1024)S(1)} %copy-done.17, f32[3072]{0:T(1024)S(1)} %broadcast_add_fusion), kind=kOutput, calls=%fused_computation.48 | convolution fusion | flops 1814298624 | bytes 17915904 | tf_op jit(solution)/shard_map/dot_general | solution.py:196
  153.3 70.6 %all-reduce.3.cloned.1.call-done = f32[256,3072]{1,0:T(8,128)} async-done(((f32[256,3072]{1,0:T(8,128)}), f32[256,3072]{1,0:T(8,128)}) %all-reduce.3.cloned.1.call-update) | async-done | bytes 3145744 | tf_op jit(solution)/shard_map/psum | solution.py:208
  223.9 2.9 fusion.26
  226.8 1.7 dynamic-slice_reduce_fusion
  228.5 1.3 fusion.30
  229.9 252.3 %psum.23 = f32[3,768]{1,0:T(4,128)} all-reduce(f32[3,768]{1,0:T(4,128)S(1)} %pad_maximum_fusion.4), channel_id=1, replica_groups=mesh['seq'=64,'head'=4] {'seq'}, use_global_device_ids=true, to_apply=%region_17.18 | all-reduce | flops 2304 | bytes 18432 | tf_op jit(solution)/shard_map/psum | solution.py:112
  482.2 1.0 reshape.197
  483.3 0.7 copy.60
  484.0 21.3 %all-reduce.5.cloned.1.call-done = f32[192,768]{1,0:T(8,128)} async-done(((f32[192,768]{1,0:T(8,128)}), f32[192,768]{1,0:T(8,128)}) %all-reduce.5.cloned.1.call-update) | async-done | bytes 589840 | tf_op jit(solution)/shard_map/psum | solution.py:112
  505.3 1.9 copy.73
  (109 shorter events, 7.6 us)
Async XLA Ops:
  8.0 19.1 %copy-start = (bf16[192,3072]{1,0:T(8,128)(2,1)S(1)}, bf16[192,3072]{1,0:T(8,128)(2,1)}, u32[]{:S(2)}) copy-start(bf16[192,3072]{1,0:T(8,128)(2,1)} %param.11) | copy-start | bytes 3538948
  8.0 215.9 %all-reduce.3.cloned.1.call-start = ((), (), s32[]{:S(2)}) async-start(), calls=%async_computation.2 | async-start | bytes 6291456 | tf_op jit(solution)/shard_map/psum | solution.py:208
  8.1 16.3 %collective-permute-start = (bf16[1,16,1024]{2,1,0:T(8,128)(2,1)}, bf16[1,16,1024]{2,1,0:T(8,128)(2,1)S(1)}, u32[]{:S(2)}, u32[]{:S(2)}) collective-permute-start(bf16[1,16,1024]{2,1,0:T(8,128)(2,1)} %param.10), channel_id=1, source_target_pairs={{0,8},{4,12},{8,16},{12,20},{16,24},{20,28},{24,32},{28,36},{32,40... | collective-permute-start | bytes 98312 | tf_op jit(solution)/shard_map/ppermute | solution.py:23
  12.0 12.3 %collective-permute-start.1 = (bf16[1,16,1024]{2,1,0:T(8,128)(2,1)}, bf16[1,16,1024]{2,1,0:T(8,128)(2,1)S(1)}, u32[]{:S(2)}, u32[]{:S(2)}) collective-permute-start(bf16[1,16,1024]{2,1,0:T(8,128)(2,1)} %param.10), channel_id=1, source_target_pairs={{8,0},{12,4},{16,8},{20,12},{24,16},{28,20},{32,24},{36,28},{40,32... | collective-permute-start | bytes 98312 | tf_op jit(solution)/shard_map/ppermute | solution.py:23
  14.0 10.3 %copy-start.18 = (bf16[1,16,1024]{2,1,0:T(8,128)(2,1)S(1)}, bf16[1,16,1024]{2,1,0:T(8,128)(2,1)}, u32[]{:S(2)}) copy-start(bf16[1,16,1024]{2,1,0:T(8,128)(2,1)} %param.10) | copy-start | bytes 98308
  24.3 2.8 copy-start.19
  27.1 3.3 slice-start.2
  27.8 1.6 copy-start.2
  27.8 3.5 slice-start.3
  29.4 1.9 copy-start.17
  31.3 2.3 copy-start.4
  31.3 3.4 copy-start.20
  33.6 1.1 copy-start.8
  33.6 1.4 copy-start.22
  33.6 1.9 copy-start.16
  33.9 6.0 %copy-start.21 = (f32[128]{0:T(128)S(1)}, f32[128]{0:T(128)}, u32[]{:S(2)}) copy-start(f32[128]{0:T(128)} %param.16) | copy-start | bytes 1540
  34.9 1.8 collective-permute-start.2
  35.6 29.5 %copy-start.15 = (bf16[2,2,1,8,8,3,128]{6,4,3,5,1,0,2:T(8,128)(2,1)}, bf16[2,2,1,8,8,3,128]{6,4,3,5,1,0,2:T(8,128)(2,1)S(1)}, u32[]{:S(2)}) copy-start(bf16[2,2,1,8,8,3,128]{6,4,3,5,1,0,2:T(8,128)(2,1)S(1)} %copy.51) | copy-start | bytes 589828
  36.9 20.9 %collective-permute-start.3 = (bf16[2,256,2,3,128]{4,1,3,2,0:T(8,128)(2,1)S(1)}, bf16[2,256,2,3,128]{4,1,3,2,0:T(8,128)(2,1)}, u32[]{:S(2)}, u32[]{:S(2)}) collective-permute-start(bf16[2,256,2,3,128]{4,1,3,2,0:T(8,128)(2,1)S(1)} %pad_maximum_fusion.2), channel_id=1, source_target_pairs={{0,8},{4,12},{8,0},{12,4},{16,24},{20,28},{24,16},{28,20},{32,40},... | collective-permute-start | bytes 2359304 | tf_op jit(solution)/shard_map/ppermute | solution.py:17
  65.1 1.7 copy-start.6
  70.8 2.1 copy-start.10
  75.2 0.9 copy-start.11
  95.7 36.6 %copy-start.12 = (bf16[4,3,64,512]{3,2,1,0:T(8,128)(2,1)S(1)}, bf16[4,3,64,512]{3,2,1,0:T(8,128)(2,1)}, u32[]{:S(2)}) copy-start(bf16[4,3,64,512]{3,2,1,0:T(8,128)(2,1)} %copy-done.11) | copy-start | bytes 2359300
  95.9 36.0 %collective-permute-start.4 = (f32[2,256,2,3,128]{4,1,3,2,0:T(8,128)S(1)}, f32[2,256,2,3,128]{4,1,3,2,0:T(8,128)S(1)}, u32[]{:S(2)}, u32[]{:S(2)}) collective-permute-start(f32[2,256,2,3,128]{4,1,3,2,0:T(8,128)S(1)} %copy.57), channel_id=1, source_target_pairs={{0,8},{4,12},{8,0},{12,4},{16,24},{20,28},{24,16},{28,20},{32,40},... | collective-permute-start | bytes 4718600 | tf_op jit(solution)/shard_map/ppermute | solution.py:17
  131.9 2.2 copy-start.7
  131.9 4.5 slice-start
  132.2 2.6 copy-start.9
  132.2 4.1 slice-start.1
  132.2 2.4 collective-permute-start.5
  135.6 0.7 copy-start.13
  135.6 0.7 copy-start.14
  140.3 4.5 copy-start.5
  140.3 341.9 %reduce-scatter.2.cloned.1.call-start = ((), (), s32[]{:S(2)}) async-start(), calls=%async_computation.1 | async-start | bytes 14376960 | tf_op jit(solution)/shard_map/reduce_scatter | solution.py:195
  153.2 70.7 %copy-start.3 = (f32[256,3072]{1,0:T(8,128)S(1)}, f32[256,3072]{1,0:T(8,128)}, u32[]{:S(2)}) copy-start(f32[256,3072]{1,0:T(8,128)} %copy-done.2) | copy-start | bytes 9437188
  153.2 352.1 %all-reduce.5.cloned.1.call-start = ((), (), s32[]{:S(2)}) async-start(), calls=%async_computation.3 | async-start | bytes 1179648 | tf_op jit(solution)/shard_map/psum | solution.py:112
  226.8 280.5 %copy-start.1 = (bf16[192,3072]{1,0:T(8,128)(2,1)S(1)}, bf16[192,3072]{1,0:T(8,128)(2,1)}, u32[]{:S(2)}) copy-start(bf16[192,3072]{1,0:T(8,128)(2,1)} %param.11) | copy-start | bytes 3538948
Sparse Core Ops, SparseCore 0:
  140.5 83.3 all-reduce.2
Sparse Core Ops, SparseCore 1:
  153.3 168.1 reduce-scatter.1
  325.3 179.9 all-reduce.4
where the time goes:
time: 516 us; the launch traced here: 515 us
  blocking collectives  252 us (49%)
  waiting for transfers between devices  145 us (28%)
  local copies, waits for them, and re-layouts  40.5 us (8%)
  other arithmetic  28 us (5%)
  matrix products  22.3 us (4%)
  between operations  16.1 us (3%)
  starting transfers between devices  10.5 us (2%)
    psum x1, blocking collectives, seq_total(): return lax.psum((stem_part, vector_part), 'seq')  252 us
    psum x1, waiting for transfers between devices, per_device(): feature_grad = lax.psum(feature_grad, 'head')  70.6 us
    ppermute x4, waiting for transfers between devices, swapped(): return lax.ppermute(value, axis, pairs)  52.9 us
    psum x1, waiting for transfers between devices, seq_total(): return lax.psum((stem_part, vector_part), 'seq')  21.3 us
    unnamed x59, local copies, waits for them, and re-layouts  20.7 us
  transfers between devices with their start and end apart: 9, of which 5 were waited for; matrix products, arithmetic and copies ran while one was open for 6% of the time, Pallas kernels for 0%

commit v1 on v0

--- a/solution.py
+++ b/solution.py
@@ -205,7 +205,8 @@
         mixed_grad, flat_weight, (((1,), (1,)), ((), ())), preferred_element_type=jnp.float32
     )
     patch_rows = patches.astype(jnp.float32)
-    feature_grad = lax.psum(feature_grad, "head")
+    shards = lax.all_gather(feature_grad, "head", axis=0, tiled=False)
+    feature_grad = shards.sum(axis=0)
     embed_grad = norm_back(feature_grad, normed, inv_std, mod_scale)
     share_cols = model_width // lax.axis_size("head")
     offset = lax.axis_index("head") * share_cols

time: 516 us -> 542 us (1.050)
  waiting for transfers between devices: 145 us -> 165 us
  other arithmetic: 28 us -> 35.9 us
    all_gather x0 -> x1, waiting for transfers between devices: none -> 112 us  [per_device(): shards = lax.all_gather(feature_grad, 'head', axis=0, tiled=False)]
    psum x1 -> x0, waiting for transfers between devices: 70.6 us -> none  [per_device(): feature_grad = lax.psum(feature_grad, 'head')]
    psum x1, waiting for transfers between devices: 21.3 us -> 0.01 us  [seq_total(): return lax.psum((stem_part, vector_part), 'seq')]
    reduce_sum x0 -> x1, other arithmetic: none -> 7.97 us  [per_device(): feature_grad = shards.sum(axis=0)]
  transfers between devices with their start and end apart: 9 -> 9, of which waited for: 5 -> 4; matrix products, arithmetic and copies ran while one was open for 6% -> 7% of each run, Pallas kernels for 0% -> 0%
where the time goes in v1:
time: 542 us; the launch traced here: 541 us
  blocking collectives  251 us (46%)
  waiting for transfers between devices  165 us (30%)
  local copies, waits for them, and re-layouts  40.5 us (7%)
  other arithmetic  35.9 us (7%)
  matrix products  22.2 us (4%)
  between operations  16.1 us (3%)
  starting transfers between devices  10.5 us (2%)
    psum x1, blocking collectives, seq_total(): return lax.psum((stem_part, vector_part), 'seq')  251 us
    all_gather x1, waiting for transfers between devices, per_device(): shards = lax.all_gather(feature_grad, 'head', axis=0, tiled=False)  112 us
    ppermute x4, waiting for transfers between devices, swapped(): return lax.ppermute(value, axis, pairs)  52.9 us
    unnamed x59, local copies, waits for them, and re-layouts  20.6 us
  transfers between devices with their start and end apart: 9, of which 4 were waited for; matrix products, arithmetic and copies ran while one was open for 7% of the time, Pallas kernels for 0%

profile of v1, /device:TPU:8, one launch (start us, length us, event | category | flops | bytes accessed | tf_op | source)
XLA Modules:
  0.0 541.3 jit_solution(2409160519575261496)
XLA Ops:
  8.1 4.0 collective-permute-start
  12.0 1.3 collective-permute-start.1
  13.3 0.7 broadcast_add_fusion
  14.0 10.3 %copy.44 = bf16[3072,3,3,128]{0,3,2,1:T(8,128)(2,1)} copy(bf16[3072,3,3,128]{3,0,2,1:T(8,128)(2,1)} %param.15) | data formatting | bytes 14155776 | tf_op args[5]
  24.7 1.7 copy.42
  26.4 0.7 reshape.189
  27.1 0.7 fusion.29
  28.3 1.2 copy-done.2
  29.5 0.5 subtract_multiply_fusion
  30.4 0.9 slice-done.3
  31.3 2.3 fusion
  34.0 0.6 copy-done.8
  35.5 1.1 collective-permute-done.2
  36.8 2.9 collective-permute-start.3
  40.1 17.6 %collective-permute-done.3 = bf16[2,256,2,3,128]{4,1,3,2,0:T(8,128)(2,1)} collective-permute-done((bf16[2,256,2,3,128]{4,1,3,2,0:T(8,128)(2,1)S(1)}, bf16[2,256,2,3,128]{4,1,3,2,0:T(8,128)(2,1)}, u32[]{:S(2)}, u32[]{:S(2)}) %collective-permute-start.3) | collective-permute-done | bytes 786464 | tf_op jit(solution)/shard_map/ppermute | solution.py:17
  57.6 1.2 broadcast_select_fusion.1
  59.6 2.6 gather_fusion
  62.2 2.3 copy.48
  64.5 0.5 copy_select_fusion
  65.0 0.7 fusion.2
  65.7 1.0 copy-done.6
  66.7 0.7 multiply_exponential_fusion
  67.4 3.4 convolution_bitcast_fusion.1
  70.8 2.1 fusion.4
  72.9 1.9 copy.54
  75.1 0.9 copy-done.11
  76.0 0.6 multiply_bitcast_fusion
  76.6 2.4 copy.53
  79.0 3.3 pad_maximum_fusion
  82.3 3.1 copy.55
  85.7 9.3 %scatter_fusion = f32[8,128,2,3,128]{4,1,3,2,0:T(8,128)S(1)} fusion(f32[8,128,2,3,128]{4,1,3,2,0:T(8,128)S(1)} %broadcast_in_dim.47, s32[16]{0:T(128)S(1)} %fusion.24, f32[16,128,2,3,128]{4,1,3,2,0:T(8,128)} %copy.55), kind=kCustom, calls=%fused_computation.1 | custom fusion | flops 1572864 | bytes 18874432 | tf_op jit(solution)/shard_map/scatter-add | solution.py:184
  95.9 1.8 collective-permute-start.4
  97.7 34.2 %collective-permute-done.4 = f32[2,256,2,3,128]{4,1,3,2,0:T(8,128)S(1)} collective-permute-done((f32[2,256,2,3,128]{4,1,3,2,0:T(8,128)S(1)}, f32[2,256,2,3,128]{4,1,3,2,0:T(8,128)S(1)}, u32[]{:S(2)}, u32[]{:S(2)}) %collective-permute-start.4) | collective-permute-done | bytes 1572896 | tf_op jit(solution)/shard_map/ppermute | solution.py:17
  132.3 1.8 copy-done.7
  135.6 0.6 copy-done.13
  136.3 3.9 convolution_bitcast_fusion
  140.5 2.1 maximum_convert_fusion
  142.5 2.1 copy.59
  144.7 8.4 %fusion.14 = f32[3072,1152]{1,0:T(8,128)} fusion(bf16[256,1152]{0,1:T(8,128)(2,1)} %bitcast.150, f32[256,3072]{1,0:T(8,128)S(1)} %copy-done.5, f32[3072]{0:T(1024)S(1)} %copy-done.17, f32[3072]{0:T(1024)S(1)} %broadcast_add_fusion), kind=kOutput, calls=%fused_computation.48 | convolution fusion | flops 1814298624 | bytes 17915904 | tf_op jit(solution)/shard_map/dot_general | solution.py:196
  153.2 112.0 %all-gather.3.cloned.1.call-done = f32[1024,3072]{1,0:T(8,128)} async-done(((f32[256,3072]{1,0:T(8,128)}), f32[1024,3072]{1,0:T(8,128)}) %all-gather.3.cloned.1.call-update) | async-done | bytes 12582928 | tf_op jit(solution)/shard_map/all_gather | solution.py:208
  265.2 8.0 %reduce_sum.142 = f32[256,3072]{1,0:T(8,128)} reduce(f32[4,256,3072]{2,1,0:T(8,128)} %bitcast.136, f32[]{:T(128)} %constant.98.clone.1), dimensions={0}, to_apply=%region_10.11 | reduce | flops 2359296 | bytes 15728644 | tf_op jit(solution)/shard_map/reduce_sum | solution.py:209
  273.1 2.8 fusion.26
  275.9 1.8 dynamic-slice_reduce_fusion
  277.7 1.3 fusion.30
  279.1 251.1 %psum.15 = f32[3,768]{1,0:T(4,128)} all-reduce(f32[3,768]{1,0:T(4,128)S(1)} %pad_maximum_fusion.4), channel_id=1, replica_groups=mesh['seq'=64,'head'=4] {'seq'}, use_global_device_ids=true, to_apply=%region_17.18 | all-reduce | flops 2304 | bytes 18432 | tf_op jit(solution)/shard_map/psum | solution.py:112
  530.2 1.0 reshape.197
  531.3 0.7 copy.60
  532.0 1.9 copy.72
  (110 shorter events, 7.5 us)
Async XLA Ops:
  8.0 19.1 %copy-start = (bf16[192,3072]{1,0:T(8,128)(2,1)S(1)}, bf16[192,3072]{1,0:T(8,128)(2,1)}, u32[]{:S(2)}) copy-start(bf16[192,3072]{1,0:T(8,128)(2,1)} %param.11) | copy-start | bytes 3538948
  8.0 257.1 %all-gather.3.cloned.1.call-start = ((), (), s32[]{:S(2)}) async-start(), calls=%async_computation.3 | async-start | bytes 15728640 | tf_op jit(solution)/shard_map/all_gather | solution.py:208
  8.1 16.3 %collective-permute-start = (bf16[1,16,1024]{2,1,0:T(8,128)(2,1)}, bf16[1,16,1024]{2,1,0:T(8,128)(2,1)S(1)}, u32[]{:S(2)}, u32[]{:S(2)}) collective-permute-start(bf16[1,16,1024]{2,1,0:T(8,128)(2,1)} %param.10), channel_id=1, source_target_pairs={{0,8},{4,12},{8,16},{12,20},{16,24},{20,28},{24,32},{28,36},{32,40... | collective-permute-start | bytes 98312 | tf_op jit(solution)/shard_map/ppermute | solution.py:23
  12.0 12.3 %collective-permute-start.1 = (bf16[1,16,1024]{2,1,0:T(8,128)(2,1)}, bf16[1,16,1024]{2,1,0:T(8,128)(2,1)S(1)}, u32[]{:S(2)}, u32[]{:S(2)}) collective-permute-start(bf16[1,16,1024]{2,1,0:T(8,128)(2,1)} %param.10), channel_id=1, source_target_pairs={{8,0},{12,4},{16,8},{20,12},{24,16},{28,20},{32,24},{36,28},{40,32... | collective-permute-start | bytes 98312 | tf_op jit(solution)/shard_map/ppermute | solution.py:23
  14.0 10.3 %copy-start.18 = (bf16[1,16,1024]{2,1,0:T(8,128)(2,1)S(1)}, bf16[1,16,1024]{2,1,0:T(8,128)(2,1)}, u32[]{:S(2)}) copy-start(bf16[1,16,1024]{2,1,0:T(8,128)(2,1)} %param.10) | copy-start | bytes 98308
  24.3 2.8 copy-start.19
  27.1 3.3 slice-start.2
  27.8 1.7 copy-start.2
  27.8 3.5 slice-start.3
  29.5 1.8 copy-start.17
  31.3 2.3 copy-start.4
  31.3 3.3 copy-start.20
  33.6 1.0 copy-start.8
  33.6 1.3 copy-start.22
  33.6 1.8 copy-start.16
  33.9 5.9 %copy-start.21 = (f32[128]{0:T(128)S(1)}, f32[128]{0:T(128)}, u32[]{:S(2)}) copy-start(f32[128]{0:T(128)} %param.16) | copy-start | bytes 1540
  34.8 1.8 collective-permute-start.2
  35.5 29.5 %copy-start.15 = (bf16[2,2,1,8,8,3,128]{6,4,3,5,1,0,2:T(8,128)(2,1)}, bf16[2,2,1,8,8,3,128]{6,4,3,5,1,0,2:T(8,128)(2,1)S(1)}, u32[]{:S(2)}) copy-start(bf16[2,2,1,8,8,3,128]{6,4,3,5,1,0,2:T(8,128)(2,1)S(1)} %copy.51) | copy-start | bytes 589828
  36.8 20.9 %collective-permute-start.3 = (bf16[2,256,2,3,128]{4,1,3,2,0:T(8,128)(2,1)S(1)}, bf16[2,256,2,3,128]{4,1,3,2,0:T(8,128)(2,1)}, u32[]{:S(2)}, u32[]{:S(2)}) collective-permute-start(bf16[2,256,2,3,128]{4,1,3,2,0:T(8,128)(2,1)S(1)} %pad_maximum_fusion.2), channel_id=1, source_target_pairs={{0,8},{4,12},{8,0},{12,4},{16,24},{20,28},{24,16},{28,20},{32,40},... | collective-permute-start | bytes 2359304 | tf_op jit(solution)/shard_map/ppermute | solution.py:17
  65.0 1.7 copy-start.6
  70.8 2.1 copy-start.10
  75.1 0.9 copy-start.11
  95.7 36.6 %copy-start.12 = (bf16[4,3,64,512]{3,2,1,0:T(8,128)(2,1)S(1)}, bf16[4,3,64,512]{3,2,1,0:T(8,128)(2,1)}, u32[]{:S(2)}) copy-start(bf16[4,3,64,512]{3,2,1,0:T(8,128)(2,1)} %copy-done.11) | copy-start | bytes 2359300
  95.9 36.0 %collective-permute-start.4 = (f32[2,256,2,3,128]{4,1,3,2,0:T(8,128)S(1)}, f32[2,256,2,3,128]{4,1,3,2,0:T(8,128)S(1)}, u32[]{:S(2)}, u32[]{:S(2)}) collective-permute-start(f32[2,256,2,3,128]{4,1,3,2,0:T(8,128)S(1)} %copy.57), channel_id=1, source_target_pairs={{0,8},{4,12},{8,0},{12,4},{16,24},{20,28},{24,16},{28,20},{32,40},... | collective-permute-start | bytes 4718600 | tf_op jit(solution)/shard_map/ppermute | solution.py:17
  131.9 2.2 copy-start.7
  131.9 4.5 slice-start
  132.2 2.6 copy-start.9
  132.2 4.1 slice-start.1
  132.2 2.4 collective-permute-start.5
  135.6 0.7 copy-start.13
  135.6 0.7 copy-start.14
  140.2 4.5 copy-start.5
  140.2 390.0 %reduce-scatter.2.cloned.1.call-start = ((), (), s32[]{:S(2)}) async-start(), calls=%async_computation.1 | async-start | bytes 14376960 | tf_op jit(solution)/shard_map/reduce_scatter | solution.py:195
  153.1 378.9 %all-reduce.2.cloned.1.call-start = ((), (), s32[]{:S(2)}) async-start(), calls=%async_computation.2 | async-start | bytes 1179648 | tf_op jit(solution)/shard_map/psum | solution.py:112
  265.2 8.0 %copy-start.3 = (f32[256,3072]{1,0:T(8,128)S(1)}, f32[256,3072]{1,0:T(8,128)}, u32[]{:S(2)}) copy-start(f32[256,3072]{1,0:T(8,128)} %copy-done.2) | copy-start | bytes 9437188
  275.9 257.9 %copy-start.1 = (bf16[192,3072]{1,0:T(8,128)(2,1)S(1)}, bf16[192,3072]{1,0:T(8,128)(2,1)}, u32[]{:S(2)}) copy-start(bf16[192,3072]{1,0:T(8,128)(2,1)} %param.11) | copy-start | bytes 3538948
Sparse Core Ops, SparseCore 0:
  140.3 124.7 all-gather.2
Sparse Core Ops, SparseCore 1:
  153.2 168.2 reduce-scatter.1
  325.4 180.1 all-reduce.1
